TPU v7x, 32 devices: a whole 2x2x4 slice. The times are simulated.
32 devices in a mesh: seq: 8 (over z, x), tp: 4 (over y, core).
Axes of the slice: x: 2, y: 2, z: 4, core: 2. Of those that a mesh axis runs over, the one named last changes fastest.
Arguments:
- conv_in: bfloat16 [1024, 16384], P('seq', 'tp'), may hold values from -6 to 6
- conv_weight: float32 [4, 16384], P(None, 'tp'), may hold values from -3 to 3
- conv_bias: float32 [16384], P('tp'), may hold values from -0.5 to 0.5
- proj_weight: bfloat16 [16384, 544], P('tp'), may hold values from -0.046875 to 0.046875
- dt_weight: bfloat16 [512, 16384], P(None, 'tp'), may hold values from -0.25 to 0.25
- dt_bias: float32 [16384], P('tp'), may hold values from -6 to -2.5
- decay_rate: float32 [16, 16384], P(None, 'tp'), may hold values from 0.0009765625 to 4
- skip_gain: float32 [16384], P('tp'), may hold values from 0.5 to 1.5
- grad_out: bfloat16 [1024, 16384], P('seq', 'tp'), may hold values from -6 to 6
Outputs:
- mixed: bfloat16 [1024, 16384], P('seq', 'tp')
- weight_grad: float32 [4, 4096, 16], P('tp', 'seq')
All inputs are finite; a program needn't handle non-finite values.
Results may differ from a plain program's by a relative error of at most 0.006.
Values may be sent and summed in bfloat16 or wider, within the bound.
No kernel may reach another device: no remote copies, remote signals or barrier semaphores. Data moves between devices by JAX's collectives and lax.ppermute only.
A program may use at most 128 MiB of HBM per device.

v0:
```python
import jax
import jax.numpy as jnp
from jax import lax
from jax.sharding import PartitionSpec as P

block_len = 16


def shifted(shard, axis, by):
    count = lax.axis_size(axis)
    pairs = [(i, i + by) for i in range(count) if 0 <= i + by < count]
    return lax.ppermute(shard, axis, pairs)


def entering(part, axis, combine, identity):
    place = lax.axis_index(axis)
    gathered = jax.tree.map(lambda a: lax.all_gather(a, axis), part)
    state = jax.tree.map(lambda a, e: jnp.zeros_like(a) + jnp.asarray(e, a.dtype), part, identity)

    def one(turn, state):
        return combine(
            state, jax.tree.map(lambda a: lax.dynamic_index_in_dim(a, turn, 0, False), gathered)
        )

    return lax.fori_loop(0, place, one, state)


def chain_pair(earlier, later):
    return (earlier[0] * later[0], later[0] * earlier[1] + later[1])


def local_pass(initial, decay_rate, slices):

    def block_step(carried, pieces):
        step_now, drive_now, b_now, c_now, grad_now = pieces
        outputs = []
        grads = []
        for offset in range(block_len):
            carried = (
                jnp.exp(-step_now[offset][None, :] * decay_rate) * carried
                + drive_now[offset][None, :] * b_now[offset][:, None]
            )
            outputs.append(jnp.sum(carried * c_now[offset][:, None], axis=0))
            grads.append(jnp.sum(carried * grad_now[offset][None, :], axis=1))
        return (carried, (jnp.stack(outputs), jnp.stack(grads)))

    return lax.scan(block_step, initial, slices)


def local_ending(step_size, drive_in, b_matrix, decay_rate):
    after = jnp.flip(jnp.cumsum(jnp.flip(step_size, 0), axis=0), 0) - step_size
    rows = []
    for state_index in range(decay_rate.shape[0]):
        weights = jnp.exp(-decay_rate[state_index][None, :] * after)
        rows.append(
            jnp.sum(weights * drive_in * b_matrix[:, state_index : state_index + 1], axis=0)
        )
    return jnp.stack(rows)


def on_device(
    conv_in,
    conv_weight,
    conv_bias,
    proj_weight,
    dt_weight,
    dt_bias,
    decay_rate,
    skip_gain,
    grad_out,
):
    tok_rows, channels = conv_in.shape
    taps = conv_weight.shape[0]
    rank_width = dt_weight.shape[0]
    states = decay_rate.shape[0]
    tok_total = tok_rows * lax.axis_size("seq")
    rim_rows = shifted(conv_in[tok_rows - (taps - 1) :], "seq", 1)
    extended = jnp.concatenate([rim_rows, conv_in], axis=0).astype(jnp.float32)
    pre_act = conv_bias[None, :] + jnp.zeros((tok_rows, channels), jnp.float32)
    for tap_index in range(taps):
        pre_act = (
            pre_act + conv_weight[tap_index][None, :] * extended[tap_index : tap_index + tok_rows]
        )
    conv_out = jax.nn.silu(pre_act).astype(jnp.bfloat16)
    partial_proj = jnp.dot(conv_out, proj_weight, preferred_element_type=jnp.float32)
    proj_out = lax.psum(partial_proj, "tp").astype(jnp.bfloat16)
    dt_low = proj_out[:, :rank_width]
    b_matrix = proj_out[:, rank_width : rank_width + states].astype(jnp.float32)
    c_matrix = proj_out[:, rank_width + states :].astype(jnp.float32)
    step_size = jax.nn.softplus(
        jnp.dot(dt_low, dt_weight, preferred_element_type=jnp.float32) + dt_bias[None, :]
    )
    drive_in = step_size * conv_out.astype(jnp.float32)
    scaled_grad = grad_out.astype(jnp.float32) / tok_total
    blocks = tok_rows // block_len
    slices = (
        step_size.reshape(blocks, block_len, channels),
        drive_in.reshape(blocks, block_len, channels),
        b_matrix.reshape(blocks, block_len, states),
        c_matrix.reshape(blocks, block_len, states),
        scaled_grad.reshape(blocks, block_len, channels),
    )
    zero_state = jnp.zeros((states, channels), jnp.float32)
    local_end = local_ending(step_size, drive_in, b_matrix, decay_rate)
    total_decay = jnp.exp(-decay_rate * jnp.sum(step_size, axis=0)[None, :])
    identity = (jnp.ones((states, channels), jnp.float32), zero_state)
    _, incoming = entering((total_decay, local_end), "seq", chain_pair, identity)
    _, (scan_out, grad_parts) = local_pass(incoming, decay_rate, slices)
    mixed = (
        scan_out.reshape(tok_rows, channels) + skip_gain[None, :] * conv_out.astype(jnp.float32)
    ).astype(jnp.bfloat16)
    grad_c = lax.psum(grad_parts.reshape(tok_rows, states), "tp").astype(jnp.bfloat16)
    weight_grad = lax.psum_scatter(
        lax.dot_general(
            conv_out, grad_c, (((0,), (0,)), ((), ())), preferred_element_type=jnp.float32
        ),
        "seq",
        scatter_dimension=0,
        tiled=True,
    )
    return (mixed, weight_grad[None])


def solution(mesh):
    return jax.shard_map(
        on_device,
        mesh=mesh,
        in_specs=(
            P("seq", "tp"),
            P(None, "tp"),
            P("tp"),
            P("tp", None),
            P(None, "tp"),
            P("tp"),
            P(None, "tp"),
            P("tp"),
            P("seq", "tp"),
        ),
        out_specs=(P("seq", "tp"), P("tp", "seq", None)),
        check_vma=False,
    )
```

profile of v0, /device:TPU:0, one launch (start us, length us, event | category | flops | bytes accessed | tf_op | source)
XLA Modules:
  0.0 394.6 jit_solution(8271281646402718323)
XLA Ops:
  8.1 4.9 %collective-permute-start = (bf16[3,4096]{1,0:T(4,128)(2,1)S(1)}, bf16[3,4096]{1,0:T(4,128)(2,1)S(1)}, u32[]{:S(2)}, u32[]{:S(2)}) collective-permute-start(bf16[3,4096]{1,0:T(4,128)(2,1)S(1)} %slice.453), channel_id=1, source_target_pairs={{0,4},{4,8},{8,12},{12,16},{16,20},{20,24},{24,28},{1,5},{5,9},{9,... | collective-permute-start | bytes 73736 | tf_op jit(solution)/shard_map/ppermute | solution.py:12
  13.0 2.4 slice_negate_fusion.15
  15.4 1.1 fusion.57
  16.5 1.7 maximum_convert_fusion
  18.2 1.3 multiply_convert_fusion
  20.5 1.3 fusion.59
  21.9 14.5 %all-reduce.1 = bf16[128,544]{0,1:T(8,128)(2,1)S(1)} all-reduce(f32[128,544]{0,1:T(8,128)S(1)} %fusion.59), channel_id=1, replica_groups=mesh['seq'=8,'tp'=4] {'tp'}, use_global_device_ids=true, to_apply=%region_0.1 | all-reduce | flops 69632 | bytes 417792 | tf_op jit(solution)/shard_map/psum | solution.py:86
  37.0 6.0 %fusion.58 = (f32[4096]{0:T(1024)}, f32[128,4096]{1,0:T(8,128)}) fusion(f32[4096]{0:T(1024)S(1)} %copy-done.14, bf16[512,4096]{1,0:T(8,128)(2,1)} %param.17, bf16[128,544]{0,1:T(8,128)(2,1)S(1)} %all-reduce.1), kind=kOutput, calls=%fused_computation.252 | convolution fusion | flops 541061120 | bytes 6455296 | tf_op jit(solution)/shard_map/dot_general | solution.py:91
  43.0 16.6 %rev.7 = f32[128,4096]{1,0:T(8,128)} reverse(f32[128,4096]{1,0:T(8,128)} %get-tuple-element.359), dimensions={0} | reverse | bytes 4194304 | tf_op jit(solution)/shard_map/jit(_flip)/rev | solution.py:51
  59.6 4.6 %reduce_window_sum.11 = f32[128,4096]{1,0:T(8,128)} reduce-window(f32[128,4096]{1,0:T(8,128)} %rev.7, f32[]{:T(128)} %constant.51.clone.1), window={size=128x1 pad=127_0x0_0}, to_apply=%region_2.3 | reduce-window | flops 66584576 | bytes 4194308 | tf_op jit(solution)/shard_map/jit(cumsum)/reduce_window_sum | solution.py:51
  64.2 16.6 %rev.8 = f32[128,4096]{1,0:T(8,128)} reverse(f32[128,4096]{1,0:T(8,128)} %reduce_window_sum.11), dimensions={0} | reverse | bytes 4194304 | tf_op jit(solution)/shard_map/jit(_flip)/rev | solution.py:51
  80.8 7.7 %multiply_reduce_fusion.32 = (f32[4096]{0:T(1024)}, f32[4096]{0:T(1024)}, f32[4096]{0:T(1024)}, f32[4096]{0:T(1024)}, f32[4096]{0:T(1024)}, /*index=5*/f32[4096]...) fusion(f32[128]{0:T(128)S(1)} %get-tuple-element.343, ...), kind=kLoop, calls=%fused_computation.195 | loop fusion | flops 25133056 | bytes 17125376 | tf_op jit(solution)/shard_map/reduce_sum | solution.py:56
  88.5 4.6 %multiply_reduce_fusion.40 = (f32[4096]{0:T(1024)}, f32[4096]{0:T(1024)}, f32[4096]{0:T(1024)}, f32[4096]{0:T(1024)}, f32[4096]{0:T(1024)}, /*index=5*/f32[4096]{0:T(1024)}, f32[4096]{0:T(1024)}, f32[4096]{0:T(1024)}) fusion(f32[128,4096]{1,0:T(8,128)S(1)} %get-tuple-element.207, f32[128,4096]{1,0:T(8,128)S(1)} %get-tuple-element.206, ...), kind=kLoop, calls=%fused_computation.203 | loop fusion | flops 16744448 | bytes 4460544 | tf_op jit(solution)/shard_map/reduce_sum | solution.py:56
  93.1 3.4 stack.169
  96.6 1.5 multiply_exponential_fusion
  98.2 1.6 convert_multiply_fusion.2
  101.4 44.3 %all-gather.7.cloned.1.call-done = f32[128,4096]{1,0:T(8,128)} async-done(((f32[16,4096]{1,0:T(8,128)}), f32[128,4096]{1,0:T(8,128)}) %all-gather.7.cloned.1.call-update) | async-done | bytes 2097168 | tf_op jit(solution)/shard_map/all_gather | solution.py:17
  145.6 49.8 %all-gather.5.cloned.1.call-done = f32[128,4096]{1,0:T(8,128)} async-done(((f32[16,4096]{1,0:T(8,128)}), f32[128,4096]{1,0:T(8,128)}) %all-gather.5.cloned.1.call-update) | async-done | bytes 2097168 | tf_op jit(solution)/shard_map/all_gather | solution.py:17
  195.7 109.5 %while.27 = (s32[]{:T(128)}, f32[16,4096]{1,0:T(8,128)S(1)}, f32[8,16,4096]{2,1,0:T(8,128)}, f32[8,16,16]{2,1,0:T(8,128)}, f32[8,16,4096]{2,1,0:T(8,128)}, /*ind...) while((s32[]{:T(128)}, f32[16,4096]{1,0:T(8,128)S(1)}, ...), condition=%wide.region_54.55_spmd, body=%wide.region_21.54_spmd.sunk | while | flops 10485521 | bytes 10244477 | solution.py:47
  195.7 3.3 constant_dynamic-slice_fusion.81
  199.2 2.4 fusion.69
  201.7 2.0 multiply_reduce_fusion.53
  204.7 1.0 multiply_reduce_fusion.55
  209.1 3.5 constant_dynamic-slice_fusion.81
  212.8 2.5 fusion.69
  215.3 2.0 multiply_reduce_fusion.53
  222.7 3.6 constant_dynamic-slice_fusion.81
  226.6 2.5 fusion.69
  229.1 2.0 multiply_reduce_fusion.53
  236.6 3.7 constant_dynamic-slice_fusion.81
  240.5 2.5 fusion.69
  243.0 2.0 multiply_reduce_fusion.53
  250.5 3.7 constant_dynamic-slice_fusion.81
  254.3 2.5 fusion.69
  256.8 2.0 multiply_reduce_fusion.53
  264.3 3.4 constant_dynamic-slice_fusion.81
  267.9 2.5 fusion.69
  270.4 2.0 multiply_reduce_fusion.53
  277.8 3.4 constant_dynamic-slice_fusion.81
  281.4 2.5 fusion.69
  283.9 2.0 multiply_reduce_fusion.53
  291.4 3.6 constant_dynamic-slice_fusion.81
  295.2 2.5 fusion.69
  297.8 2.0 multiply_reduce_fusion.53
  305.2 11.2 %psum.15 = bf16[128,16]{1,0:T(8,128)(2,1)S(1)} all-reduce(f32[128,16]{1,0:T(8,128)} %bitcast.509), channel_id=1, replica_groups=mesh['seq'=8,'tp'=4] {'tp'}, use_global_device_ids=true, to_apply=%region_55.56 | all-reduce | flops 2048 | bytes 12288 | tf_op jit(solution)/shard_map/psum | solution.py:112
  316.4 2.2 fusion.60
  318.7 4.0 %fusion.49 = bf16[128,4096]{1,0:T(8,128)(2,1)} fusion(f32[8,16,4096]{2,1,0:T(8,128)} %get-tuple-element.100, f32[4096]{0:T(1024)} %param.20, f32[131,4096]{1,0:T(8,128)S(1)} %maximum_convert_fusion, f32[4096]{0:T(1024)S(1)} %bitcast.503, f32[4096]{0:T(1024)S(1)} %bitcast.506, f32[4096]{0:T(1024)S(1)} %bitcast.500, f32[4096]{0:T(1024)S(1)} %bitcast.497, ...), kind=kLoop, calls=%fused_computation.185 | loop fusion | flops 8912896 | bytes 11632640 | tf_op jit(solution)/shard_map/convert_element_type | solution.py:111
  322.7 65.4 %reduce-scatter.2.cloned.1.call-done = f32[512,16]{0,1:T(8,128)} async-done(((f32[4096,16]{0,1:T(8,128)}), f32[512,16]{0,1:T(8,128)}) %reduce-scatter.2.cloned.1.call-update) | async-done | bytes 32784 | tf_op jit(solution)/shard_map/reduce_scatter | solution.py:113
  (144 shorter events, 48.5 us)
Async XLA Ops:
  7.2 11.0 %copy-start.10 = (f32[4096]{0:T(1024)S(1)}, f32[4096]{0:T(1024)}, u32[]{:S(2)}) copy-start(f32[4096]{0:T(1024)} %param.15) | copy-start | bytes 49156
  7.2 138.5 %all-gather.7.cloned.1.call-start = ((), (), s32[]{:S(2)}) async-start(), calls=%async_computation.3 | async-start | bytes 2359296 | tf_op jit(solution)/shard_map/all_gather | solution.py:17
  8.1 8.4 %collective-permute-start = (bf16[3,4096]{1,0:T(4,128)(2,1)S(1)}, bf16[3,4096]{1,0:T(4,128)(2,1)S(1)}, u32[]{:S(2)}, u32[]{:S(2)}) collective-permute-start(bf16[3,4096]{1,0:T(4,128)(2,1)S(1)} %slice.453), channel_id=1, source_target_pairs={{0,4},{4,8},{8,12},{12,16},{16,20},{20,24},{24,28},{1,5},{5,9},{9,... | collective-permute-start | bytes 73736 | tf_op jit(solution)/shard_map/ppermute | solution.py:12
  16.5 64.3 %copy-start.4 = (f32[1,4096]{1,0:T(1,128)}, f32[1,4096]{1,0:T(1,128)S(1)}, u32[]{:S(2)}) copy-start(f32[1,4096]{1,0:T(1,128)S(1)} %get-tuple-element.339) | copy-start | bytes 49156
  16.5 64.3 %copy-start.6 = (f32[1,4096]{1,0:T(1,128)}, f32[1,4096]{1,0:T(1,128)S(1)}, u32[]{:S(2)}) copy-start(f32[1,4096]{1,0:T(1,128)S(1)} %get-tuple-element.340) | copy-start | bytes 49156
  16.5 64.3 %copy-start.8 = (f32[1,4096]{1,0:T(1,128)}, f32[1,4096]{1,0:T(1,128)S(1)}, u32[]{:S(2)}) copy-start(f32[1,4096]{1,0:T(1,128)S(1)} %get-tuple-element.341) | copy-start | bytes 49156
  16.5 4.0 %slice-start = ((s8[4456448]{0:T(1024)(128)(4,1)}), s8[4194304]{0:T(1024)(128)(4,1)S(1)}, s32[]{:S(2)}) async-start(s8[4456448]{0:T(1024)(128)(4,1)} %bitcast.411), calls=%async_computation.4 | async-start | bytes 8388608
  18.2 2.3 slice-start.1
  19.6 1.0 copy-start.1
  20.5 16.4 %copy-start.14 = (f32[4096]{0:T(1024)S(1)}, f32[4096]{0:T(1024)}, u32[]{:S(2)}) copy-start(f32[4096]{0:T(1024)} %param.18) | copy-start | bytes 49156
  37.0 6.0 %copy-start.12 = (f32[128,16]{0,1:T(8,128)}, f32[128,16]{0,1:T(8,128)S(1)}, u32[]{:S(2)}) copy-start(f32[128,16]{0,1:T(8,128)S(1)} %get-tuple-element.337) | copy-start | bytes 24580
  88.5 4.6 %copy-start.2 = (f32[128,4096]{1,0:T(8,128)}, f32[128,4096]{1,0:T(8,128)S(1)}, u32[]{:S(2)}) copy-start(f32[128,4096]{1,0:T(8,128)S(1)} %get-tuple-element.207) | copy-start | bytes 6291460
  88.5 8.1 %copy-start = (f32[16,4096]{1,0:T(8,128)S(1)}, f32[16,4096]{1,0:T(8,128)}, u32[]{:S(2)}) copy-start(f32[16,4096]{1,0:T(8,128)} %param.19) | copy-start | bytes 786436
  93.1 5.1 %copy-start.3 = (bf16[128,4096]{1,0:T(8,128)(2,1)S(1)}, bf16[128,4096]{1,0:T(8,128)(2,1)}, u32[]{:S(2)}) copy-start(bf16[128,4096]{1,0:T(8,128)(2,1)} %param.21) | copy-start | bytes 3145732
  96.6 98.8 %all-gather.5.cloned.1.call-start = ((), (), s32[]{:S(2)}) async-start(), calls=%async_computation.2 | async-start | bytes 2359296 | tf_op jit(solution)/shard_map/all_gather | solution.py:17
  98.1 290.0 %reduce-scatter.2.cloned.1.call-start = ((), (), s32[]{:S(2)}) async-start(), calls=%async_computation.1 | async-start | bytes 294912 | tf_op jit(solution)/shard_map/reduce_scatter | solution.py:113
  195.7 123.0 %copy-start.5 = (f32[1,4096]{1,0:T(1,128)S(1)}, f32[1,4096]{1,0:T(1,128)}, u32[]{:S(2)}) copy-start(f32[1,4096]{1,0:T(1,128)} %copy-done.4) | copy-start | bytes 49156
  195.7 123.0 %copy-start.7 = (f32[1,4096]{1,0:T(1,128)S(1)}, f32[1,4096]{1,0:T(1,128)}, u32[]{:S(2)}) copy-start(f32[1,4096]{1,0:T(1,128)} %copy-done.6) | copy-start | bytes 49156
  195.7 123.0 %copy-start.9 = (f32[1,4096]{1,0:T(1,128)S(1)}, f32[1,4096]{1,0:T(1,128)}, u32[]{:S(2)}) copy-start(f32[1,4096]{1,0:T(1,128)} %copy-done.8) | copy-start | bytes 49156
  195.7 123.0 %copy-start.11 = (f32[4096]{0:T(1024)S(1)}, f32[4096]{0:T(1024)}, u32[]{:S(2)}) copy-start(f32[4096]{0:T(1024)} %param.15) | copy-start | bytes 49156
  203.6 3.0 copy-start.13
  217.3 3.0 copy-start.13
  231.1 3.0 copy-start.13
  245.0 3.0 copy-start.13
  258.8 3.0 copy-start.13
  272.4 3.0 copy-start.13
  285.9 3.0 copy-start.13
  299.7 3.0 copy-start.13
Sparse Core Ops, SparseCore 0:
  96.7 48.8 all-gather.6
  147.8 47.6 all-gather.4
  318.8 69.2 reduce-scatter.1
where the time goes:
time: 398 us; the launch traced here: 395 us
  waiting for transfers between devices  159 us (40%)
  local copies, waits for them, and re-layouts  90.4 us (23%)
  other arithmetic  89.8 us (23%)
  blocking collectives  25.7 us (6%)
  between operations  14 us (4%)
  matrix products  9.51 us (2%)
  starting transfers between devices  4.99 us (1%)
    all_gather x2, waiting for transfers between devices, entering(): gathered = jax.tree.map(lambda a: lax.all_gather(a, axis), part)  94 us
    reduce_scatter x1, waiting for transfers between devices, on_device(): lax.psum_scatter(lax.dot_general(conv_out, grad_c, (((0,), (0,)), ((), ()...  65.4 us
    reduce_sum x40, other arithmetic, block_step(): grads.append(jnp.sum(carried * grad_now[offset][None, :], axis=1))  39.7 us
    rev x2, local copies, waits for them, and re-layouts, local_ending(): after = jnp.flip(jnp.cumsum(jnp.flip(step_size, 0), axis=0), 0) - step_size  33.2 us
    slice x8, local copies, waits for them, and re-layouts, block_step(): grads.append(jnp.sum(carried * grad_now[offset][None, :], axis=1))  28.2 us
    neg x8, other arithmetic, block_step(): -step_now[offset][None, :] * decay_rate  20 us
    psum x1, blocking collectives, on_device(): proj_out = lax.psum(partial_proj, 'tp').astype(jnp.bfloat16)  14.5 us
    reduce_sum x2, other arithmetic, local_ending(): jnp.sum(weights * drive_in * b_matrix[:, state_index:state_index + 1], ax...  12.3 us
  transfers between devices with their start and end apart: 4, of which 3 were waited for; matrix products, arithmetic and copies ran while one was open for 3% of the time, Pallas kernels for 0%

commit v1 on v0

--- a/solution.py
+++ b/solution.py
@@ -83,7 +83,7 @@
         )
     conv_out = jax.nn.silu(pre_act).astype(jnp.bfloat16)
     partial_proj = jnp.dot(conv_out, proj_weight, preferred_element_type=jnp.float32)
-    proj_out = lax.psum(partial_proj, "tp").astype(jnp.bfloat16)
+    proj_out = jnp.sum(lax.all_gather(partial_proj, "tp"), axis=0).astype(jnp.bfloat16)
     dt_low = proj_out[:, :rank_width]
     b_matrix = proj_out[:, rank_width : rank_width + states].astype(jnp.float32)
     c_matrix = proj_out[:, rank_width + states :].astype(jnp.float32)

time: 398 us -> 414 us (1.040)
  waiting for transfers between devices: 159 us -> 180 us
  blocking collectives: 25.7 us -> 10.7 us
  other arithmetic: 89.8 us -> 99.8 us
    all_gather x0 -> x1, waiting for transfers between devices: none -> 18.9 us  [on_device(): lax.all_gather(partial_proj, 'tp')]
    psum x1 -> x0, blocking collectives: 14.5 us -> none  [on_device(): proj_out = lax.psum(partial_proj, 'tp').astype(jnp.bfloat16)]
    reduce_sum x40, other arithmetic: 39.7 us -> 51.3 us  [block_step(): grads.append(jnp.sum(carried * grad_now[offset][None, :], axis=1))]
    another operation x16, local copies, waits for them, and re-layouts: 8.92 us -> 14.6 us  [block_step(): return (carried, (jnp.stack(outputs), jnp.stack(grads)))]
    dynamic_update_slice x16, local copies, waits for them, and re-layouts: 10.6 us -> 5.86 us  [local_pass(): return lax.scan(block_step, initial, slices)]
  transfers between devices with their start and end apart: 4 -> 5, of which waited for: 3 -> 5; matrix products, arithmetic and copies ran while one was open for 3% -> 2% of each run, Pallas kernels for 0% -> 0%
where the time goes in v1:
time: 414 us; the launch traced here: 411 us
  waiting for transfers between devices  180 us (43%)
  other arithmetic  99.8 us (24%)
  local copies, waits for them, and re-layouts  90.8 us (22%)
  between operations  14 us (3%)
  blocking collectives  10.7 us (3%)
  matrix products  9.62 us (2%)
  starting transfers between devices  5.22 us (1%)
    all_gather x2, waiting for transfers between devices, entering(): gathered = jax.tree.map(lambda a: lax.all_gather(a, axis), part)  95.1 us
    reduce_scatter x1, waiting for transfers between devices, on_device(): lax.psum_scatter(lax.dot_general(conv_out, grad_c, (((0,), (0,)), ((), ()...  65.3 us
    reduce_sum x40, other arithmetic, block_step(): grads.append(jnp.sum(carried * grad_now[offset][None, :], axis=1))  51.3 us
    rev x2, local copies, waits for them, and re-layouts, local_ending(): after = jnp.flip(jnp.cumsum(jnp.flip(step_size, 0), axis=0), 0) - step_size  33.3 us
    slice x8, local copies, waits for them, and re-layouts, block_step(): grads.append(jnp.sum(carried * grad_now[offset][None, :], axis=1))  28.2 us
    neg x8, other arithmetic, block_step(): -step_now[offset][None, :] * decay_rate  20 us
    all_gather x1, waiting for transfers between devices, on_device(): lax.all_gather(partial_proj, 'tp')  18.9 us
    another operation x16, local copies, waits for them, and re-layouts, block_step(): return (carried, (jnp.stack(outputs), jnp.stack(grads)))  14.6 us
  transfers between devices with their start and end apart: 5, of which 5 were waited for; matrix products, arithmetic and copies ran while one was open for 2% of the time, Pallas kernels for 0%

profile of v1, /device:TPU:0, one launch (start us, length us, event | category | flops | bytes accessed | tf_op | source)
XLA Modules:
  0.0 410.7 jit_solution(11681784516430478369)
XLA Ops:
  8.1 4.9 %collective-permute-start = (bf16[3,4096]{1,0:T(4,128)(2,1)S(1)}, bf16[3,4096]{1,0:T(4,128)(2,1)S(1)}, u32[]{:S(2)}, u32[]{:S(2)}) collective-permute-start(bf16[3,4096]{1,0:T(4,128)(2,1)S(1)} %slice.453), channel_id=1, source_target_pairs={{0,4},{4,8},{8,12},{12,16},{16,20},{20,24},{24,28},{1,5},{5,9},{9,... | collective-permute-start | bytes 73736 | tf_op jit(solution)/shard_map/ppermute | solution.py:12
  14.5 1.7 maximum_convert_fusion
  18.6 2.0 fusion.59
  21.2 18.9 %all-gather.7.cloned.1.call-done = f32[512,544]{0,1:T(8,128)} async-done(((f32[128,544]{0,1:T(8,128)}), f32[512,544]{0,1:T(8,128)}) %all-gather.7.cloned.1.call-update) | async-done | bytes 1114128 | tf_op jit(solution)/shard_map/all_gather | solution.py:86
  40.0 2.6 reshape.346
  42.7 1.9 reduce_sum.450
  44.6 5.4 %fusion.58 = (f32[4096]{0:T(1024)S(1)}, f32[128,4096]{1,0:T(8,128)}) fusion(f32[4096]{0:T(1024)S(1)} %copy-done.4, bf16[512,4096]{1,0:T(8,128)(2,1)} %param.17, bf16[128,544]{0,1:T(8,128)(2,1)S(1)} %reduce_sum.450), kind=kOutput, calls=%fused_computation.252 | convolution fusion | flops 541061120 | bytes 6455296 | tf_op jit(solution)/shard_map/dot_general | solution.py:91
  50.0 16.6 %rev.7 = f32[128,4096]{1,0:T(8,128)} reverse(f32[128,4096]{1,0:T(8,128)} %get-tuple-element.349), dimensions={0} | reverse | bytes 4194304 | tf_op jit(solution)/shard_map/jit(_flip)/rev | solution.py:51
  66.6 4.6 %reduce_window_sum.11 = f32[128,4096]{1,0:T(8,128)} reduce-window(f32[128,4096]{1,0:T(8,128)} %rev.7, f32[]{:T(128)} %constant.51.clone.1), window={size=128x1 pad=127_0x0_0}, to_apply=%region_2.3 | reduce-window | flops 66584576 | bytes 4194308 | tf_op jit(solution)/shard_map/jit(cumsum)/reduce_window_sum | solution.py:51
  71.3 16.6 %rev.8 = f32[128,4096]{1,0:T(8,128)} reverse(f32[128,4096]{1,0:T(8,128)} %reduce_window_sum.11), dimensions={0} | reverse | bytes 4194304 | tf_op jit(solution)/shard_map/jit(_flip)/rev | solution.py:51
  87.9 7.0 %multiply_reduce_fusion.32 = (f32[4096]{0:T(1024)S(1)}, f32[4096]{0:T(1024)S(1)}, f32[4096]{0:T(1024)S(1)}, f32[4096]{0:T(1024)S(1)}, f32[4096]{0:T(1024)S(1)}, ...) fusion(f32[128]{0:T(128)S(1)} %get-tuple-element.333, ...), kind=kLoop, calls=%fused_computation.195 | loop fusion | flops 25133056 | bytes 17125376 | tf_op jit(solution)/shard_map/reduce_sum | solution.py:56
  95.0 4.0 multiply_reduce_fusion.40
  99.0 1.7 stack.169
  101.6 2.8 convert_multiply_fusion.2
  104.6 45.4 %all-gather.11.cloned.1.call-done = f32[128,4096]{1,0:T(8,128)} async-done(((f32[16,4096]{1,0:T(8,128)}), f32[128,4096]{1,0:T(8,128)}) %all-gather.11.cloned.1.call-update) | async-done | bytes 2097168 | tf_op jit(solution)/shard_map/all_gather | solution.py:17
  149.9 49.8 %all-gather.9.cloned.1.call-done = f32[128,4096]{1,0:T(8,128)} async-done(((f32[16,4096]{1,0:T(8,128)}), f32[128,4096]{1,0:T(8,128)}) %all-gather.9.cloned.1.call-update) | async-done | bytes 2097168 | tf_op jit(solution)/shard_map/all_gather | solution.py:17
  200.0 121.9 %while.27 = (s32[]{:T(128)}, f32[16,4096]{1,0:T(8,128)S(1)}, f32[8,16,4096]{2,1,0:T(8,128)}, f32[8,16,16]{2,1,0:T(8,128)S(1)}, f32[8,16,4096]{2,1,0:T(8,128)}, /...) while((s32[]{:T(128)}, f32[16,4096]{1,0:T(8,128)S(1)}, ...), condition=%wide.region_54.55_spmd, body=%wide.region_21.54_spmd.sunk | while | flops 10485521 | bytes 10250853 | solution.py:47
  200.0 3.3 constant_dynamic-slice_fusion.81
  203.5 2.4 fusion.69
  205.9 2.0 multiply_reduce_fusion.53
  212.3 1.4 stack.173
  214.9 3.5 constant_dynamic-slice_fusion.81
  218.6 2.5 fusion.69
  221.1 2.0 multiply_reduce_fusion.53
  227.5 1.4 stack.173
  230.1 3.6 constant_dynamic-slice_fusion.81
  233.9 2.5 fusion.69
  236.4 2.0 multiply_reduce_fusion.53
  245.5 3.7 constant_dynamic-slice_fusion.81
  249.4 2.5 fusion.69
  251.9 2.0 multiply_reduce_fusion.53
  260.9 3.7 constant_dynamic-slice_fusion.81
  264.8 2.5 fusion.69
  267.3 2.0 multiply_reduce_fusion.53
  276.3 3.4 constant_dynamic-slice_fusion.81
  279.9 2.5 fusion.69
  282.4 2.0 multiply_reduce_fusion.53
  288.8 1.4 stack.173
  291.4 3.4 constant_dynamic-slice_fusion.81
  295.0 2.5 fusion.69
  297.5 2.0 multiply_reduce_fusion.53
  306.5 3.6 constant_dynamic-slice_fusion.81
  310.3 2.5 fusion.69
  312.9 2.0 multiply_reduce_fusion.53
  321.9 10.7 %psum.7 = bf16[128,16]{1,0:T(8,128)(2,1)S(1)} all-reduce(f32[128,16]{1,0:T(8,128)S(1)} %bitcast.511), channel_id=1, replica_groups=mesh['seq'=8,'tp'=4] {'tp'}, use_global_device_ids=true, to_apply=%region_55.56 | all-reduce | flops 2048 | bytes 12288 | tf_op jit(solution)/shard_map/psum | solution.py:112
  332.5 2.2 fusion.60
  334.8 4.0 fusion.49
  338.8 65.3 %reduce-scatter.2.cloned.1.call-done = f32[512,16]{0,1:T(8,128)} async-done(((f32[4096,16]{0,1:T(8,128)}), f32[512,16]{0,1:T(8,128)}) %reduce-scatter.2.cloned.1.call-update) | async-done | bytes 32784 | tf_op jit(solution)/shard_map/reduce_scatter | solution.py:113
  (114 shorter events, 59.8 us)
Async XLA Ops:
  7.2 9.1 %copy-start.3 = (f32[4096]{0:T(1024)S(1)}, f32[4096]{0:T(1024)}, u32[]{:S(2)}) copy-start(f32[4096]{0:T(1024)} %param.15) | copy-start | bytes 49156
  7.2 32.9 %all-gather.7.cloned.1.call-start = ((), (), s32[]{:S(2)}) async-start(), calls=%async_computation.2 | async-start | bytes 1392640 | tf_op jit(solution)/shard_map/all_gather | solution.py:86
  8.1 6.5 %collective-permute-start = (bf16[3,4096]{1,0:T(4,128)(2,1)S(1)}, bf16[3,4096]{1,0:T(4,128)(2,1)S(1)}, u32[]{:S(2)}, u32[]{:S(2)}) collective-permute-start(bf16[3,4096]{1,0:T(4,128)(2,1)S(1)} %slice.453), channel_id=1, source_target_pairs={{0,4},{4,8},{8,12},{12,16},{16,20},{20,24},{24,28},{1,5},{5,9},{9,... | collective-permute-start | bytes 73736 | tf_op jit(solution)/shard_map/ppermute | solution.py:12
  14.5 4.0 slice-start
  16.2 2.3 slice-start.1
  17.6 1.0 copy-start.1
  18.6 2.3 copy-start
  20.6 24.0 %copy-start.4 = (f32[4096]{0:T(1024)S(1)}, f32[4096]{0:T(1024)}, u32[]{:S(2)}) copy-start(f32[4096]{0:T(1024)} %param.18) | copy-start | bytes 49156
  20.6 129.3 %all-gather.11.cloned.1.call-start = ((), (), s32[]{:S(2)}) async-start(), calls=%async_computation.4 | async-start | bytes 2359296 | tf_op jit(solution)/shard_map/all_gather | solution.py:17
  95.0 4.0 copy-start.2
  100.7 99.0 %all-gather.9.cloned.1.call-start = ((), (), s32[]{:S(2)}) async-start(), calls=%async_computation.3 | async-start | bytes 2359296 | tf_op jit(solution)/shard_map/all_gather | solution.py:17
  101.5 302.6 %reduce-scatter.2.cloned.1.call-start = ((), (), s32[]{:S(2)}) async-start(), calls=%async_computation.1 | async-start | bytes 294912 | tf_op jit(solution)/shard_map/reduce_scatter | solution.py:113
Sparse Core Ops, SparseCore 0:
  20.7 19.2 all-gather.6
  100.8 49.0 all-gather.10
  152.1 47.6 all-gather.8
  334.9 69.1 reduce-scatter.1
